TPU v7x, 32 devices: a whole 2x2x4 slice. The times are simulated.
32 devices in a mesh: kz: 4 (over x, core), en: 2 (over y), sp: 4 (over z).
Axes of the slice: x: 2, y: 2, z: 4, core: 2. Of those that a mesh axis runs over, the one named last changes fastest.
Arguments:
- green: float32 [4, 4, 4, 2, 256, 256], P('kz', 'en', 'sp'), may hold values from -0.1 to 0.1
- coupling: float32 [4, 3, 256, 256], P('sp'), may hold values from -0.375 to 0.375
- phonon_weight: float32 [3], replicated, may hold values from 0.2 to 0.6
- mode_index: int32 [4, 5], P('kz'), may hold values from 0 to 2
- onsite: float32 [4, 256], P('sp'), may hold values from 0.8 to 1.2
- hopping: float32 [4, 256], P('sp'), may hold values from 0.45 to 0.95
- energies: float32 [4], P('en'), may hold values from -0.1 to 0.1
- guess_scale: float32 [4, 4, 4], P('kz', 'en', 'sp'), may hold values from 0.45 to 0.75
Outputs:
- boundary: float32 [4, 4, 4, 2, 256, 256], P('kz', 'en', 'sp')
All inputs are finite; a program needn't handle non-finite values.
Results may differ from a plain program's by a relative error of at most 0.0003.
Values sent between devices are 32-bit elements; how exact they have to be, the bound alone decides.
A program may use at most 64 MiB of HBM per device.

v0:
```python
import jax
import jax.numpy as jnp
from jax import lax
from jax.sharding import PartitionSpec as P

REACH = 2
NEWTON = 3


HIGHEST_PRECISION = lax.Precision.HIGHEST


def with_halo(cells, sides, width):
    for axis, dim in sides:
        count = lax.axis_size(axis)
        ends = count - 1
        head = lax.slice_in_dim(cells, 0, width, axis=dim)
        tail = lax.slice_in_dim(cells, cells.shape[dim] - width, cells.shape[dim], axis=dim)
        cells = jnp.concatenate(
            [
                lax.ppermute(tail, axis, [(i, (i + 1) % count) for i in range(ends)]),
                cells,
                lax.ppermute(head, axis, [((i + 1) % count, i) for i in range(ends)]),
            ],
            axis=dim,
        )
    return cells


def entering(value, axis, combine, identity):
    size, position = (lax.axis_size(axis), lax.axis_index(axis))
    everything = jax.tree.map(lambda part: lax.all_gather(part, axis), value)
    start = jax.tree.map(
        lambda part, zero: jnp.broadcast_to(jnp.asarray(zero, part.dtype), part.shape),
        value,
        identity,
    )

    def lap(k, before):
        reached = k < position
        new = combine(before, jax.tree.map(lambda part: part[k], everything))
        return jax.tree.map(lambda a, b: jnp.where(reached, a, b), new, before)

    return lax.fori_loop(0, size, lap, start)


def sandwich(matrix, blocks):
    left_product = jnp.einsum("ab,nbc->nac", matrix, blocks, precision=HIGHEST_PRECISION)
    return jnp.einsum("nac,dc->nad", left_product, matrix, precision=HIGHEST_PRECISION)


def batched(first, second):
    return jnp.einsum("...ab,...bc->...ac", first, second, precision=HIGHEST_PRECISION)


def chain_combine(earlier, later):
    outer_hop = later[0][:, None] * later[0][None, :]
    return (earlier[0] * later[0], outer_hop * earlier[1] + later[1])


def body(green, coupling, phonon_weight, mode_index, onsite, hopping, energies, guess_scale):
    energy_count = green.shape[1]
    orbitals = green.shape[-1]
    local_green = green.reshape(energy_count * 2, orbitals, orbitals)
    couplings = coupling[0]
    mode_range = jnp.arange(couplings.shape[0], dtype=jnp.int32)

    def scatter_term(running, blocks, column):
        selector = (mode_index[0, column] == mode_range).astype(jnp.float32)
        matrix = jnp.sum(selector[:, None, None] * couplings, axis=0)
        weight = jnp.sum(selector * phonon_weight)
        return running + weight * sandwich(matrix, blocks)

    scattered = scatter_term(jnp.zeros(local_green.shape, jnp.float32), local_green, REACH)
    gathered = lax.all_gather(local_green[None], "kz", axis=0, tiled=True)
    point_count = lax.axis_size("kz")
    position = lax.axis_index("kz")
    for distance in range(1, REACH + 1):
        for direction in (1, -1):
            source = (position - direction * distance + point_count * REACH) % point_count
            shifted = lax.dynamic_index_in_dim(gathered, source, 0, keepdims=False)
            scattered = scatter_term(scattered, shifted, REACH + direction * distance)
    scattered = scattered.reshape(energy_count, 2, orbitals, orbitals)
    padded = with_halo(scattered, (("en", 0),), 1)
    self_energy = padded[:-2] + padded[2:]
    identity = jnp.eye(orbitals, dtype=jnp.float32)
    diagonal_shift = onsite[0][None, :] - energies[:, None]
    system_re = self_energy[:, 0] + identity * diagonal_shift[:, None, :]
    system_im = self_energy[:, 1]
    guess = guess_scale[0, :, 0][:, None, None]
    inverse_re = 2.0 * guess * identity - guess * guess * system_re
    inverse_im = -(guess * guess) * system_im
    for step in range(NEWTON - 1):
        product_re = batched(system_re, inverse_re) - batched(system_im, inverse_im)
        product_im = batched(system_re, inverse_im) + batched(system_im, inverse_re)
        residual_re = 2.0 * identity - product_re
        residual_im = -product_im
        inverse_re, inverse_im = (
            batched(inverse_re, residual_re) - batched(inverse_im, residual_im),
            batched(inverse_re, residual_im) + batched(inverse_im, residual_re),
        )
    inverse = jnp.stack([inverse_re, inverse_im], axis=1)
    hop_slab = hopping[0]
    prefix_hops, prefix = entering(
        (hop_slab, inverse), "sp", chain_combine, (jnp.ones_like(hop_slab), jnp.zeros_like(inverse))
    )
    outer_hop = hop_slab[:, None] * hop_slab[None, :]
    boundary = outer_hop * prefix + inverse
    return boundary.reshape(1, energy_count, 1, 2, orbitals, orbitals)


def solution(mesh):
    placed = (
        P("kz", "en", "sp", None, None, None),
        P("sp", None, None, None),
        P(),
        P("kz", None),
        P("sp", None),
        P("sp", None),
        P("en"),
        P("kz", "en", "sp"),
    )
    return jax.shard_map(
        body,
        mesh=mesh,
        in_specs=placed,
        out_specs=P("kz", "en", "sp", None, None, None),
        check_vma=False,
    )
```

profile of v0, /device:TPU:0, one launch (start us, length us, event | category | flops | bytes accessed | tf_op | source)
XLA Modules:
  0.0 186.6 jit_solution(16342872812464006514)
XLA Ops:
  7.4 1.5 fusion.84
  9.5 1.3 compare_convert_fusion
  10.8 1.1 compare_convert_fusion.2
  11.9 4.4 %fusion.73 = (f32[]{:T(128)}, f32[]{:T(128)}, f32[]{:T(128)}, f32[]{:T(128)}, f32[]{:T(128)}) fusion(f32[3]{0:T(128)} %param.12, s32[]{:T(128)} %bitcast.22, s32[]{:T(128)} %bitcast.14, s32[]{:T(128)} %bitcast.9, s32[]{:T(128)} %bitcast.4, s32[]{:T(128)} %bitcast.18), kind=kLoop, calls=%fused_computation.123 | loop fusion | flops 40 | bytes 52 | tf_op jit(solution)/shard_map/reduce_sum | solution.py:71
  16.3 1.7 fusion.27
  18.7 1.0 convolution_bitcast_fusion.4
  19.8 1.6 convolution_multiply_fusion.4
  21.4 24.7 %all-gather.5.cloned.1.call-done = f32[4,4,256,256]{3,2,1,0:T(8,128)} async-done(((f32[1,4,256,256]{3,2,1,0:T(8,128)}), f32[4,4,256,256]{3,2,1,0:T(8,128)}) %all-gather.5.cloned.1.call-update) | async-done | bytes 4194320 | tf_op jit(solution)/shard_map/all_gather | solution.py:75
  46.1 2.5 %convolution_bitcast_fusion.3 = f32[4,256,256]{2,1,0:T(8,128)S(1)} fusion(f32[4,4,256,256]{3,2,1,0:T(8,128)} %all-gather.5.cloned.1.call-done, s32[]{:T(128)S(6)} %select_n.55, f32[256,256]{1,0:T(8,128)S(1)} %get-tuple-element.129), kind=kOutput, calls=%fused_computation.9 | convolution fusion | flops 805306368 | bytes 2359300 | tf_op jit(solution)/shard_map/ab,nbc->nac/dot_general | solution.py:48
  48.6 1.6 fusion.5
  50.2 1.1 convolution_bitcast_fusion.2
  51.3 1.6 fusion.4
  53.0 1.1 convolution_bitcast_fusion.1
  54.1 1.7 fusion.3
  55.9 1.1 convolution_bitcast_fusion
  57.0 1.7 fusion.2
  58.7 3.6 %collective-permute-start = (f32[1,2,256,256]{3,2,1,0:T(8,128)S(1)}, f32[1,2,256,256]{3,2,1,0:T(8,128)S(1)}, u32[]{:S(2)}, u32[]{:S(2)}) collective-permute-start(f32[1,2,256,256]{3,2,1,0:T(8,128)S(1)} %get-tuple-element.148), channel_id=1, source_target_pairs={{0,4},{1,5},{2,6},{3,7},{8,12},{9,13},{10,14},{11,15},{16,20},{17,... | collective-permute-start | bytes 1572872 | tf_op jit(solution)/shard_map/ppermute | solution.py:21
  62.3 1.3 collective-permute-start.1
  63.7 9.9 %collective-permute-done = f32[1,2,256,256]{3,2,1,0:T(8,128)S(1)} collective-permute-done((f32[1,2,256,256]{3,2,1,0:T(8,128)S(1)}, f32[1,2,256,256]{3,2,1,0:T(8,128)S(1)}, u32[]{:S(2)}, u32[]{:S(2)}) %collective-permute-start) | collective-permute-done | bytes 524320 | tf_op jit(solution)/shard_map/ppermute | solution.py:21
  73.7 4.3 %collective-permute-done.1 = f32[1,2,256,256]{3,2,1,0:T(8,128)S(1)} collective-permute-done((f32[1,2,256,256]{3,2,1,0:T(8,128)S(1)}, f32[1,2,256,256]{3,2,1,0:T(8,128)S(1)}, u32[]{:S(2)}, u32[]{:S(2)}) %collective-permute-start.1) | collective-permute-done | bytes 524320 | tf_op jit(solution)/shard_map/ppermute | solution.py:23
  78.9 0.8 fusion.36
  79.7 0.8 fusion.10
  82.1 0.8 fusion.34
  89.7 1.0 pad_maximum_fusion.2
  90.8 10.9 %all-gather.1 = f32[4,1,256]{2,1,0:T(1,128)S(1)} all-gather(f32[1,1,256]{2,1,0:T(1,128)S(1)} %bitcast.173), channel_id=1, replica_groups=mesh['kz'=4,'en'=2,'sp'=4] {'sp'}, dimensions={0}, use_global_device_ids=true | all-gather | bytes 5120 | tf_op jit(solution)/shard_map/all_gather | solution.py:32
  101.8 69.0 %all-gather.7.cloned.1.call-done = f32[8,2,256,256]{3,2,0,1:T(8,128)} async-done(((f32[2,2,256,256]{3,2,0,1:T(8,128)}), f32[8,2,256,256]{3,2,0,1:T(8,128)}) %all-gather.7.cloned.1.call-update) | async-done | bytes 4194320 | tf_op jit(solution)/shard_map/all_gather | solution.py:32
  170.8 7.7 %while.14 = (s32[]{:T(128)}, f32[2,2,256,256]{3,2,1,0:T(8,128)S(1)}, s32[]{:T(128)}, f32[4,256]{1,0:T(4,128)S(1)}, f32[4,2,2,256,256]{4,3,1,0,2:T(8,128)}, /*index=5*/s32[]{:T(128)}, s32[]{:T(128)}) while((s32[]{:T(128)}, f32[2,2,256,256]{3,2,1,0:T(8,128)S(1)}, s32[]{:T(128)}, f32[4,256]{1,0:T(4,128)S(1)}, ...), condition=%wide.region_11.12_spmd.clone, body=%wide.region_10.11_spmd.clone.sunk | while | flops 1114116 | bytes 3673701 | solution.py:44
  170.9 1.8 fusion.111
  172.8 1.8 fusion.111
  174.8 1.8 fusion.111
  176.7 1.8 fusion.111
  178.7 1.0 copy.22
  (49 shorter events, 12.2 us)
Async XLA Ops:
  6.5 12.2 %copy-start.1 = (f32[1,2,1,2,256,256]{5,4,3,2,1,0:T(8,128)S(1)}, f32[1,2,1,2,256,256]{5,4,3,2,1,0:T(8,128)}, u32[]{:S(2)}) copy-start(f32[1,2,1,2,256,256]{5,4,3,2,1,0:T(8,128)} %param.10) | copy-start | bytes 3145732
  6.5 39.6 %all-gather.5.cloned.1.call-start = ((), (), s32[]{:S(2)}) async-start(), calls=%async_computation | async-start | bytes 5242880 | tf_op jit(solution)/shard_map/all_gather | solution.py:75
  7.3 163.5 %all-gather.7.cloned.1.call-start = ((), (), s32[]{:S(2)}) async-start(), calls=%async_computation.1 | async-start | bytes 5242880 | tf_op jit(solution)/shard_map/all_gather | solution.py:32
  46.1 4.1 %copy-start = (f32[4,4,256,256]{3,2,1,0:T(8,128)S(1)}, f32[4,4,256,256]{3,2,1,0:T(8,128)}, u32[]{:S(2)}) copy-start(f32[4,4,256,256]{3,2,1,0:T(8,128)} %all-gather.5.cloned.1.call-done) | copy-start | bytes 12582916
  55.8 7.8 %copy-start.5 = (f32[1,2,1]{1,2,0:T(1,128)S(1)}, f32[1,2,1]{1,2,0:T(1,128)}, u32[]{:S(2)}) copy-start(f32[1,2,1]{1,2,0:T(1,128)} %param.17) | copy-start | bytes 28
  55.8 7.8 %copy-start.3 = (f32[1,256]{1,0:T(1,128)S(1)}, f32[1,256]{1,0:T(1,128)}, u32[]{:S(2)}) copy-start(f32[1,256]{1,0:T(1,128)} %param.14) | copy-start | bytes 3076
  55.8 7.8 %copy-start.4 = (f32[2]{0:T(128)S(1)}, f32[2]{0:T(128)}, u32[]{:S(2)}) copy-start(f32[2]{0:T(128)} %param.16) | copy-start | bytes 28
  58.7 14.9 %collective-permute-start = (f32[1,2,256,256]{3,2,1,0:T(8,128)S(1)}, f32[1,2,256,256]{3,2,1,0:T(8,128)S(1)}, u32[]{:S(2)}, u32[]{:S(2)}) collective-permute-start(f32[1,2,256,256]{3,2,1,0:T(8,128)S(1)} %get-tuple-element.148), channel_id=1, source_target_pairs={{0,4},{1,5},{2,6},{3,7},{8,12},{9,13},{10,14},{11,15},{16,20},{17,... | collective-permute-start | bytes 1572872 | tf_op jit(solution)/shard_map/ppermute | solution.py:21
  62.3 15.7 %collective-permute-start.1 = (f32[1,2,256,256]{3,2,1,0:T(8,128)S(1)}, f32[1,2,256,256]{3,2,1,0:T(8,128)S(1)}, u32[]{:S(2)}, u32[]{:S(2)}) collective-permute-start(f32[1,2,256,256]{3,2,1,0:T(8,128)S(1)} %get-tuple-element.149), channel_id=1, source_target_pairs={{4,0},{5,1},{6,2},{7,3},{12,8},{13,9},{14,10},{15,11},{20,16},{21,... | collective-permute-start | bytes 1572872 | tf_op jit(solution)/shard_map/ppermute | solution.py:23
  87.7 3.1 %copy-start.2 = (f32[1,256]{1,0:T(1,128)S(1)}, f32[1,256]{1,0:T(1,128)}, u32[]{:S(2)}) copy-start(f32[1,256]{1,0:T(1,128)} %param.15) | copy-start | bytes 3076
Sparse Core Ops, SparseCore 0:
  8.9 37.1 all-gather.4
  90.9 79.8 all-gather.6
where the time goes:
time: 187 us
  waiting for transfers between devices  109 us (58%)
  matrix products  26.5 us (14%)
  other arithmetic  18.9 us (10%)
  between operations  13.8 us (7%)
  blocking collectives  10.9 us (6%)
  starting transfers between devices  4.93 us (3%)
  local copies, waits for them, and re-layouts  2.64 us (1%)
    all_gather x1, waiting for transfers between devices, entering(): everything = jax.tree.map(lambda part: lax.all_gather(part, axis), value)  69 us
    all_gather x1, waiting for transfers between devices, body(): gathered = lax.all_gather(local_green[None], 'kz', axis=0, tiled=True)  24.7 us
    dot_general x16, matrix products, batched(): jnp.einsum('...ab,...bc->...ac', first, second, precision=HIGHEST_PRECISION)  11.5 us
    all_gather x1, blocking collectives, entering(): everything = jax.tree.map(lambda part: lax.all_gather(part, axis), value)  10.9 us
    ppermute x1, waiting for transfers between devices, with_halo(): lax.ppermute(tail, axis, [(i, (i + 1) % count) for i in range(ends)])  9.91 us
    dot_general x5, matrix products, sandwich(): jnp.einsum('nac,dc->nad', left_product, matrix, precision=HIGHEST_PRECISION)  8.31 us
    select_n x4, other arithmetic, lap(): return jax.tree.map(lambda a, b: jnp.where(reached, a, b), new, before)  7.18 us
    dot_general x5, matrix products, sandwich(): jnp.einsum('ab,nbc->nac', matrix, blocks, precision=HIGHEST_PRECISION)  6.76 us
  transfers between devices with their start and end apart: 4, of which 4 were waited for; matrix products, arithmetic and copies ran while one was open for 8% of the time, Pallas kernels for 0%

commit v1 on v0

v1 whole, which is shorter than its diff:
```python
import functools

import jax
import jax.numpy as jnp
from jax import lax
from jax.experimental import pallas as pl
from jax.experimental.pallas import tpu as pltpu
from jax.sharding import PartitionSpec as P

REACH = 2
ROW_BLOCKS = 4
MESH = pl.DeviceIdType.MESH

SIBLING, BACK, PASSED, AHEAD = range(4)


def split(value):
    high = value.astype(jnp.bfloat16)
    return high, (value - high.astype(jnp.float32)).astype(jnp.bfloat16)


def dot_split(first, second):
    left = jnp.concatenate([first[0], first[0], first[1]], axis=1)
    right = jnp.concatenate([second[0], second[1], second[0]], axis=0)
    return jnp.dot(left, right, preferred_element_type=jnp.float32)


def complex_pair(re, im):
    return jnp.concatenate(
        [jnp.concatenate([re, -im], axis=1), jnp.concatenate([im, re], axis=1)], axis=0
    )


def kernel(
    sizes,
    mode_ref, weight_ref, energy_ref, guess_ref,
    green_ref, coupling_ref, onsite_ref, hopping_ref,
    out_ref,
    halo, own, arrived, total, inverse, before, outer,
    coup_hi, coup_lo, coupt_hi, coupt_lo,
    halo_send, halo_recv, kz_send, kz_recv, sp_send, sp_recv,
):
    kz_count, en_count, sp_count = sizes
    energy_count, _, n, _ = green_ref.shape
    ring = kz_count > 2 * REACH
    rows = n // ROW_BLOCKS
    pieces = 2 * ROW_BLOCKS
    k, en, sp = lax.axis_index("kz"), lax.axis_index("en"), lax.axis_index("sp")
    odd = lax.rem(k, 2)
    sibling = k + 1 - 2 * odd
    back = lax.rem(k + kz_count - REACH, kz_count)
    ahead = lax.rem(k + REACH, kz_count)

    barrier = pltpu.get_barrier_semaphore()

    def greet(axis, index):
        pl.semaphore_signal(barrier, inc=1, device_id={axis: index}, device_id_type=MESH)

    greet("kz", sibling)
    greet("kz", back)
    if ring:
        greet("kz", ahead)
    for axis, here, count in (("en", en, en_count), ("sp", sp, sp_count)):
        pl.when(here > 0)(lambda axis=axis, here=here: greet(axis, here - 1))
        pl.when(here < count - 1)(lambda axis=axis, here=here: greet(axis, here + 1))
    expected = 2 + int(ring)
    for here, count in ((en, en_count), (sp, sp_count)):
        expected = expected + (here > 0).astype(jnp.int32) + (here < count - 1).astype(jnp.int32)
    pl.semaphore_wait(barrier, expected)

    def remote(source, target, send, recv, axis, index):
        return pltpu.make_async_remote_copy(
            src_ref=source, dst_ref=target, send_sem=send, recv_sem=recv,
            device_id={axis: index}, device_id_type=MESH,
        )

    def halo_up(p):
        return remote(green_ref.at[energy_count - 1, p], halo.at[0, p],
                      halo_send.at[0, p], halo_recv.at[0, p], "en", en + 1)

    def halo_down(p):
        return remote(green_ref.at[0, p], halo.at[1, p],
                      halo_send.at[1, p], halo_recv.at[1, p], "en", en - 1)

    for p in range(2):
        pl.when(en < en_count - 1)(lambda p=p: halo_up(p).start())
        pl.when(en > 0)(lambda p=p: halo_down(p).start())

    @pl.when(en == 0)
    def _():
        halo[0] = jnp.zeros_like(halo[0])

    @pl.when(en == en_count - 1)
    def _():
        halo[1] = jnp.zeros_like(halo[1])

    def energy_of(i):
        return lax.rem(i + en, energy_count)

    def kz_copy(slot, i, p, source, index):
        return remote(source, arrived.at[slot, i, p], kz_send.at[slot, i, p],
                      kz_recv.at[slot, i, p], "kz", index)

    def to_back(i, p):
        slot = AHEAD if ring else BACK
        return kz_copy(slot, i, p, own.at[i, p], back)

    def to_ahead(i, p):
        return kz_copy(BACK, i, p, own.at[i, p], ahead)

    def to_sibling(i, p):
        return kz_copy(SIBLING, i, p, own.at[i, p], sibling)

    def passing(i, p):
        slot = jnp.where(odd == 1, BACK, AHEAD) if ring else BACK
        return kz_copy(PASSED, i, p, arrived.at[slot, i, p], sibling)

    def issue(i, p):
        e = energy_of(i)

        @pl.when(e > 0)
        def _():
            own[i, p] = green_ref[jnp.maximum(e - 1, 0), p]

        @pl.when(e == 0)
        def _():
            pl.when(en > 0)(lambda: halo_up(p).wait_recv())
            own[i, p] = halo[0, p]

        @pl.when(e < energy_count - 1)
        def _():
            own[i, p] += green_ref[jnp.minimum(e + 1, energy_count - 1), p]

        @pl.when(e == energy_count - 1)
        def _():
            pl.when(en < en_count - 1)(lambda: halo_down(p).wait_recv())
            own[i, p] += halo[1, p]

        to_ahead(i, p).start()
        if ring:
            to_back(i, p).start()
        to_sibling(i, p).start()

    def term(i, p, block, column, first=False):
        mode = mode_ref[column]
        matrix = (coup_hi[mode], coup_lo[mode])
        turned = (coupt_hi[mode], coupt_lo[mode])
        left = dot_split(matrix, split(block)) * weight_ref[mode]
        value = dot_split(split(left), turned)
        if first:
            total[i, p] = value
        else:
            total[i, p] += value

    def own_terms(i, p):
        term(i, p, own[i, p], REACH, first=True)

    def sibling_terms(i, p):
        to_sibling(i, p).wait_recv()
        term(i, p, arrived[SIBLING, i, p], 2 * REACH - 1 - 2 * (1 - odd))

    def pass_on(i, p):
        to_ahead(i, p).wait_recv()
        if ring:
            to_back(i, p).wait_recv()
        passing(i, p).start()

    def far_terms(i, p, between):
        term(i, p, arrived[BACK, i, p], 2 * REACH)
        between()
        term(i, p, arrived[AHEAD if ring else BACK, i, p], 0)
        between()

    def passed_terms(i, p):
        passing(i, p).wait_recv()
        term(i, p, arrived[PASSED, i, p], 2 * REACH - 1 - 2 * odd)

    def link(i, j):
        p, r = j // ROW_BLOCKS, lax.rem(j, ROW_BLOCKS)
        at = pl.ds(pl.multiple_of(r * rows, rows), rows)
        return remote(out_ref.at[energy_of(i), p, at], before.at[i, p, at],
                      sp_send.at[i, j], sp_recv.at[i, j], "sp", sp + 1)

    def chain_step(i, j):
        p, r = j // ROW_BLOCKS, lax.rem(j, ROW_BLOCKS)
        at = pl.ds(pl.multiple_of(r * rows, rows), rows)
        e = energy_of(i)

        @pl.when(sp > 0)
        def _():
            link(i, j).wait_recv()
            out_ref[e, p, at] = outer[at] * before[i, p, at] + inverse[i, p, at]

        @pl.when(sp == 0)
        def _():
            out_ref[e, p, at] = inverse[i, p, at]

        @pl.when(sp < sp_count - 1)
        def _():
            link(i, j).start()

    def invert(i, between):
        e = energy_of(i)
        guess = guess_ref[e]
        shift = onsite_ref[...] - energy_ref[e]
        diagonal = (lax.broadcasted_iota(jnp.int32, (n, n), 0)
                    == lax.broadcasted_iota(jnp.int32, (n, n), 1))
        r_re = jnp.where(diagonal, 1.0 - guess * shift, 0.0) - guess * total[i, 0]
        r_im = -guess * total[i, 1]

        def stack(re, im):
            return tuple(
                jnp.concatenate([a, b], axis=0) for a, b in zip(split(re), split(im))
            )

        def left(re, im):
            return tuple(complex_pair(a, b) for a, b in zip(split(re), split(im)))

        r_left = left(r_re, r_im)
        square = dot_split(r_left, stack(r_re, r_im))
        between()
        s_re, s_im = square[:n], square[n:]
        s_stack = stack(s_re, s_im)
        cube = dot_split(r_left, s_stack)
        fourth = dot_split(left(s_re, s_im), s_stack)
        between()
        one = jnp.where(diagonal, 1.0, 0.0)
        p_re = one + r_re + s_re + cube[:n]
        p_im = r_im + s_im + cube[n:]
        tail = dot_split(left(p_re, p_im), stack(fourth[:n], fourth[n:]))
        inverse[i, 0] = guess * (p_re + tail[:n])
        inverse[i, 1] = guess * (p_im + tail[n:])

    for p in range(2):
        issue(0, p)
    for mode in range(coupling_ref.shape[0]):
        matrix = coupling_ref[mode]
        coup_hi[mode], coup_lo[mode] = split(matrix)
        coupt_hi[mode], coupt_lo[mode] = split(matrix.T)
    across = jnp.broadcast_to(hopping_ref[...], (n, n))
    outer[...] = across * across.T

    pending = []

    def between():
        if pending:
            i, t = pending[0]
            j = t - sp

            @pl.when((sp > 0) & (j >= 0) & (j < pieces))
            def _():
                chain_step(i, j)

            pending[0] = (i, t + 1)

    def finish():
        if pending:
            i, t = pending.pop()

            @pl.loop(t, pieces + sp_count - 1)
            def _(t):
                j = t - sp

                @pl.when((sp > 0) & (j >= 0) & (j < pieces))
                def _():
                    chain_step(i, j)

    for p in range(2):
        own_terms(0, p)
        sibling_terms(0, p)
    for i in range(energy_count):
        last = i == energy_count - 1
        for p in range(2):
            if not last:
                issue(i + 1, p)
            if i == 0 or p == 1:
                pass_on(i, p)
            if not last:
                own_terms(i + 1, p)
            far_terms(i, p, between)
            if not last:
                sibling_terms(i + 1, p)
            passed_terms(i, p)
            between()
        if not last:
            called = []

            def early(i=i, called=called):
                between()
                if called:
                    pass_on(i + 1, 0)
                called.append(1)

            invert(i, early)
            finish()

            @pl.when(sp == 0)
            def _():
                @pl.loop(0, pieces)
                def _(j):
                    chain_step(i, j)

            pending.append((i, 1))
        else:
            invert(i, between)
            finish()

            @pl.loop(0, pieces)
            def _(j):
                chain_step(i, j)

    for p in range(2):
        pl.when(en < en_count - 1)(lambda p=p: halo_up(p).wait_send())
        pl.when(en > 0)(lambda p=p: halo_down(p).wait_send())
    for i in range(energy_count):
        for p in range(2):
            to_ahead(i, p).wait_send()
            if ring:
                to_back(i, p).wait_send()
            to_sibling(i, p).wait_send()
            passing(i, p).wait_send()

        @pl.when(sp < sp_count - 1)
        def _():
            @pl.loop(0, pieces)
            def _(j):
                link(i, j).wait_send()


def body(sizes, green, coupling, phonon_weight, mode_index, onsite, hopping, energies, guess_scale):
    energy_count, n = green.shape[1], green.shape[-1]
    modes = coupling.shape[1]
    blocks = (energy_count, 2, n, n)
    slots = 4 if sizes[0] > 2 * REACH else 3
    pieces = 2 * ROW_BLOCKS
    smem = pl.BlockSpec(memory_space=pltpu.SMEM)
    vmem = pl.BlockSpec(memory_space=pltpu.VMEM)
    half = pltpu.VMEM((modes, n, n), jnp.bfloat16)
    out = pl.pallas_call(
        functools.partial(kernel, sizes),
        out_shape=jax.ShapeDtypeStruct(blocks, jnp.float32),
        in_specs=[smem] * 4 + [vmem] * 4,
        out_specs=vmem,
        scratch_shapes=[
            pltpu.VMEM((2, 2, n, n), jnp.float32),
            pltpu.VMEM(blocks, jnp.float32),
            pltpu.VMEM((slots,) + blocks, jnp.float32),
            pltpu.VMEM(blocks, jnp.float32),
            pltpu.VMEM(blocks, jnp.float32),
            pltpu.VMEM(blocks, jnp.float32),
            pltpu.VMEM((n, n), jnp.float32),
            half, half, half, half,
            pltpu.SemaphoreType.DMA((2, 2)),
            pltpu.SemaphoreType.DMA((2, 2)),
            pltpu.SemaphoreType.DMA((slots, energy_count, 2)),
            pltpu.SemaphoreType.DMA((slots, energy_count, 2)),
            pltpu.SemaphoreType.DMA((energy_count, pieces)),
            pltpu.SemaphoreType.DMA((energy_count, pieces)),
        ],
        compiler_params=pltpu.CompilerParams(
            collective_id=0, has_side_effects=True, vmem_limit_bytes=50 << 20
        ),
    )(
        mode_index[0], phonon_weight, energies, guess_scale.reshape(energy_count),
        green.reshape(blocks), coupling[0], onsite, hopping,
    )
    return out.reshape(1, energy_count, 1, 2, n, n)


def solution(mesh):
    placed = (
        P("kz", "en", "sp", None, None, None),
        P("sp", None, None, None),
        P(),
        P("kz", None),
        P("sp", None),
        P("sp", None),
        P("en"),
        P("kz", "en", "sp"),
    )
    sizes = tuple(mesh.shape[axis] for axis in ("kz", "en", "sp"))
    return jax.shard_map(
        functools.partial(body, sizes),
        mesh=mesh,
        in_specs=placed,
        out_specs=P("kz", "en", "sp", None, None, None),
        check_vma=False,
    )
```

time: 187 us -> 57.4 us (0.31)
  the two profiles are of different devices: /device:TPU:0 before, /device:TPU:24 now
where the time goes in v1:
time: 57.4 us; the launch traced here: 57.2 us
  Pallas kernels  53.2 us (93%)
  local copies, waits for them, and re-layouts  4.04 us (7%)
    pallas_call x1, Pallas kernels, body(): pl.pallas_call(functools.partial(kernel, sizes), out_shape=jax.ShapeDtype...  53.2 us
    unnamed x17, local copies, waits for them, and re-layouts  4.04 us

profile of v1, /device:TPU:24, one launch (start us, length us, event | category | flops | bytes accessed | tf_op | source)
XLA Modules:
  0.0 57.2 jit_solution(8255377379889772759)
XLA Ops:
  0.0 0.0 copy-start.7
  0.0 0.0 copy-start.3
  0.0 0.0 copy-start.5
  0.0 0.0 copy-start.6
  0.0 0.0 copy-start.2
  0.0 0.0 copy-start.4
  0.0 0.6 %copy-done.7 = f32[1,2,1]{1,2,0:T(1,128)S(1)} copy-done((f32[1,2,1]{1,2,0:T(1,128)S(1)}, f32[1,2,1]{1,2,0:T(1,128)}, u32[]{:S(2)}) %copy-start.7) | copy-done | bytes 32
  0.7 0.0 copy-done.3
  0.7 0.0 copy-done.5
  0.7 0.0 copy-done.6
  0.7 0.0 copy-done.2
  0.7 0.0 copy-done.4
  0.7 0.0 copy-start
  0.7 1.2 %copy-done = f32[1,2,1,2,256,256]{5,4,3,2,1,0:T(8,128)S(1)} copy-done((f32[1,2,1,2,256,256]{5,4,3,2,1,0:T(8,128)S(1)}, f32[1,2,1,2,256,256]{5,4,3,2,1,0:T(8,128)}, u32[]{:S(2)}) %copy-start) | copy-done | bytes 1048600
  2.0 0.0 copy-start.1
  2.0 1.1 %copy-done.1 = f32[1,3,256,256]{3,2,1,0:T(8,128)S(1)} copy-done((f32[1,3,256,256]{3,2,1,0:T(8,128)S(1)}, f32[1,3,256,256]{3,2,1,0:T(8,128)}, u32[]{:S(2)}) %copy-start.1) | copy-done | bytes 786456
  3.1 53.2 %shard_map.82 = f32[2,2,256,256]{3,2,1,0:T(8,128)S(1)} custom-call(s32[5]{0:T(128)S(1)} %bitcast.10, f32[3]{0:T(128)S(1)} %copy-done.5, f32[2]{0:T(128)S(1)} %copy-done.6, f32[2]{0:T(128)S(1)} %bitcast.11, f32[2,2,256,256]{3,2,1,0:T(8,128)S(1)} %bitcast.8, f32[3,256,256]{2,1,0:T(8,128)S(1)} %bitcast.9, f32[1,256]{1,0:T(1,128)S(1)} %copy-done.2, ...), custom_call_target="tpu_custom_call" | custom-call | tf_op jit(solution)/shard_map/pallas_call | solution.py:339
  56.3 1.0 %copy.11 = f32[1,2,1,2,256,256]{5,4,3,2,1,0:T(8,128)} copy(f32[1,2,1,2,256,256]{5,4,3,2,1,0:T(8,128)S(1)} %bitcast.7) | data formatting | bytes 2097152
Async XLA Ops:
  0.0 0.7 %copy-start.7 = (f32[1,2,1]{1,2,0:T(1,128)S(1)}, f32[1,2,1]{1,2,0:T(1,128)}, u32[]{:S(2)}) copy-start(f32[1,2,1]{1,2,0:T(1,128)} %param.15) | copy-start | bytes 28
  0.0 0.7 %copy-start.3 = (f32[1,256]{1,0:T(1,128)S(1)}, f32[1,256]{1,0:T(1,128)}, u32[]{:S(2)}) copy-start(f32[1,256]{1,0:T(1,128)} %hopping_ref.1) | copy-start | bytes 3076
  0.0 0.7 %copy-start.5 = (f32[3]{0:T(128)S(1)}, f32[3]{0:T(128)}, u32[]{:S(2)}) copy-start(f32[3]{0:T(128)} %weight_ref.1) | copy-start | bytes 40
  0.0 0.7 %copy-start.6 = (f32[2]{0:T(128)S(1)}, f32[2]{0:T(128)}, u32[]{:S(2)}) copy-start(f32[2]{0:T(128)} %energy_ref.1) | copy-start | bytes 28
  0.0 0.7 %copy-start.2 = (f32[1,256]{1,0:T(1,128)S(1)}, f32[1,256]{1,0:T(1,128)}, u32[]{:S(2)}) copy-start(f32[1,256]{1,0:T(1,128)} %onsite_ref.1) | copy-start | bytes 3076
  0.0 0.7 %copy-start.4 = (s32[1,5]{1,0:T(1,128)S(1)}, s32[1,5]{1,0:T(1,128)}, u32[]{:S(2)}) copy-start(s32[1,5]{1,0:T(1,128)} %param.11) | copy-start | bytes 64
  0.7 1.2 %copy-start = (f32[1,2,1,2,256,256]{5,4,3,2,1,0:T(8,128)S(1)}, f32[1,2,1,2,256,256]{5,4,3,2,1,0:T(8,128)}, u32[]{:S(2)}) copy-start(f32[1,2,1,2,256,256]{5,4,3,2,1,0:T(8,128)} %param.8) | copy-start | bytes 3145732
  2.0 1.1 %copy-start.1 = (f32[1,3,256,256]{3,2,1,0:T(8,128)S(1)}, f32[1,3,256,256]{3,2,1,0:T(8,128)}, u32[]{:S(2)}) copy-start(f32[1,3,256,256]{3,2,1,0:T(8,128)} %param.9) | copy-start | bytes 2359300

commit v2 on v1

--- a/solution.py
+++ b/solution.py
@@ -8,7 +8,9 @@
 from jax.sharding import PartitionSpec as P
 
 REACH = 2
-ROW_BLOCKS = 4
+ROW_BLOCKS = 8
+SHARES = 2
+PACE = 2
 MESH = pl.DeviceIdType.MESH
 
 SIBLING, BACK, PASSED, AHEAD = range(4)
@@ -33,23 +35,41 @@
 
 def kernel(
     sizes,
-    mode_ref, weight_ref, energy_ref, guess_ref,
-    green_ref, coupling_ref, onsite_ref, hopping_ref,
+    mode_in, weight_in, energy_in, guess_in, green_in, coupling_in, onsite_in, hopping_in,
     out_ref,
+    mode_ref, weight_ref, energy_ref, guess_ref, green_ref, coupling_ref, onsite_ref, hopping_ref,
     halo, own, arrived, total, inverse, before, outer,
     coup_hi, coup_lo, coupt_hi, coupt_lo,
-    halo_send, halo_recv, kz_send, kz_recv, sp_send, sp_recv,
+    small_sem, coupling_sem, green_sem, halo_send, halo_recv, kz_send, kz_recv, sp_send, sp_recv,
 ):
     kz_count, en_count, sp_count = sizes
     energy_count, _, n, _ = green_ref.shape
     ring = kz_count > 2 * REACH
     rows = n // ROW_BLOCKS
+    share = n // SHARES
     pieces = 2 * ROW_BLOCKS
     k, en, sp = lax.axis_index("kz"), lax.axis_index("en"), lax.axis_index("sp")
     odd = lax.rem(k, 2)
     sibling = k + 1 - 2 * odd
     back = lax.rem(k + kz_count - REACH, kz_count)
     ahead = lax.rem(k + REACH, kz_count)
+
+    def green_load(e, p):
+        return pltpu.make_async_copy(green_in.at[e, p], green_ref.at[e, p], green_sem.at[e, p])
+
+    for p in range(2):
+        for e in range(energy_count):
+            green_load(e, p).start()
+    small_loads = [
+        pltpu.make_async_copy(source, target, small_sem.at[index])
+        for index, (source, target) in enumerate((
+            (mode_in, mode_ref), (weight_in, weight_ref), (energy_in, energy_ref),
+            (guess_in, guess_ref), (onsite_in, onsite_ref), (hopping_in, hopping_ref),
+        ))
+    ]
+    coupling_load = pltpu.make_async_copy(coupling_in, coupling_ref, coupling_sem)
+    for load in small_loads + [coupling_load]:
+        load.start()
 
     barrier = pltpu.get_barrier_semaphore()
 
@@ -75,11 +95,11 @@
         )
 
     def halo_up(p):
-        return remote(green_ref.at[energy_count - 1, p], halo.at[0, p],
+        return remote(green_in.at[energy_count - 1, p], halo.at[0, p],
                       halo_send.at[0, p], halo_recv.at[0, p], "en", en + 1)
 
     def halo_down(p):
-        return remote(green_ref.at[0, p], halo.at[1, p],
+        return remote(green_in.at[0, p], halo.at[1, p],
                       halo_send.at[1, p], halo_recv.at[1, p], "en", en - 1)
 
     for p in range(2):
@@ -97,26 +117,29 @@
     def energy_of(i):
         return lax.rem(i + en, energy_count)
 
-    def kz_copy(slot, i, p, source, index):
-        return remote(source, arrived.at[slot, i, p], kz_send.at[slot, i, p],
-                      kz_recv.at[slot, i, p], "kz", index)
-
-    def to_back(i, p):
-        slot = AHEAD if ring else BACK
-        return kz_copy(slot, i, p, own.at[i, p], back)
-
-    def to_ahead(i, p):
-        return kz_copy(BACK, i, p, own.at[i, p], ahead)
-
-    def to_sibling(i, p):
-        return kz_copy(SIBLING, i, p, own.at[i, p], sibling)
-
-    def passing(i, p):
+    def kz_copy(slot, i, p, h, source, index):
+        at = pl.ds(h * share, share)
+        return remote(source.at[i, p, at], arrived.at[slot, i, p, at], kz_send.at[slot, i, p, h],
+                      kz_recv.at[slot, i, p, h], "kz", index)
+
+    def to_back(i, p, h):
+        return kz_copy(AHEAD if ring else BACK, i, p, h, own, back)
+
+    def to_ahead(i, p, h):
+        return kz_copy(BACK, i, p, h, own, ahead)
+
+    def to_sibling(i, p, h):
+        return kz_copy(SIBLING, i, p, h, own, sibling)
+
+    def passing(i, p, h):
         slot = jnp.where(odd == 1, BACK, AHEAD) if ring else BACK
-        return kz_copy(PASSED, i, p, arrived.at[slot, i, p], sibling)
+        return kz_copy(PASSED, i, p, h, arrived.at[slot], sibling)
 
     def issue(i, p):
         e = energy_of(i)
+        if i == 0:
+            for other in range(energy_count):
+                green_load(other, p).wait()
 
         @pl.when(e > 0)
         def _():
@@ -136,10 +159,12 @@
             pl.when(en < en_count - 1)(lambda: halo_down(p).wait_recv())
             own[i, p] += halo[1, p]
 
-        to_ahead(i, p).start()
-        if ring:
-            to_back(i, p).start()
-        to_sibling(i, p).start()
+        for h in range(SHARES):
+            to_ahead(i, p, h).start()
+            if ring:
+                to_back(i, p, h).start()
+        for h in range(SHARES):
+            to_sibling(i, p, h).start()
 
     def term(i, p, block, column, first=False):
         mode = mode_ref[column]
@@ -156,14 +181,16 @@
         term(i, p, own[i, p], REACH, first=True)
 
     def sibling_terms(i, p):
-        to_sibling(i, p).wait_recv()
+        for h in range(SHARES):
+            to_sibling(i, p, h).wait_recv()
         term(i, p, arrived[SIBLING, i, p], 2 * REACH - 1 - 2 * (1 - odd))
 
     def pass_on(i, p):
-        to_ahead(i, p).wait_recv()
-        if ring:
-            to_back(i, p).wait_recv()
-        passing(i, p).start()
+        for h in range(SHARES):
+            to_ahead(i, p, h).wait_recv()
+            if ring:
+                to_back(i, p, h).wait_recv()
+            passing(i, p, h).start()
 
     def far_terms(i, p, between):
         term(i, p, arrived[BACK, i, p], 2 * REACH)
@@ -172,7 +199,8 @@
         between()
 
     def passed_terms(i, p):
-        passing(i, p).wait_recv()
+        for h in range(SHARES):
+            passing(i, p, h).wait_recv()
         term(i, p, arrived[PASSED, i, p], 2 * REACH - 1 - 2 * odd)
 
     def link(i, j):
@@ -199,7 +227,7 @@
         def _():
             link(i, j).start()
 
-    def invert(i, between):
+    def invert(i, between, emit):
         e = energy_of(i)
         guess = guess_ref[e]
         shift = onsite_ref[...] - energy_ref[e]
@@ -227,12 +255,18 @@
         one = jnp.where(diagonal, 1.0, 0.0)
         p_re = one + r_re + s_re + cube[:n]
         p_im = r_im + s_im + cube[n:]
-        tail = dot_split(left(p_re, p_im), stack(fourth[:n], fourth[n:]))
-        inverse[i, 0] = guess * (p_re + tail[:n])
-        inverse[i, 1] = guess * (p_im + tail[n:])
+        re, im = split(p_re), split(p_im)
+        fourth = stack(fourth[:n], fourth[n:])
+        sides = [(a, -b) for a, b in zip(re, im)], list(zip(im, re))
+        for p, (side, whole) in enumerate(zip(sides, (p_re, p_im))):
+            rows_left = tuple(jnp.concatenate(pair, axis=1) for pair in side)
+            inverse[i, p] = guess * (whole + dot_split(rows_left, fourth))
+            emit(p)
 
     for p in range(2):
         issue(0, p)
+    for load in small_loads + [coupling_load]:
+        load.wait()
     for mode in range(coupling_ref.shape[0]):
         matrix = coupling_ref[mode]
         coup_hi[mode], coup_lo[mode] = split(matrix)
@@ -242,28 +276,32 @@
 
     pending = []
 
+    def paced(i, t):
+        group = t - sp
+
+        @pl.when((sp > 0) & (group >= 0) & (group < pieces // PACE))
+        def _():
+            for step in range(PACE):
+                chain_step(i, group * PACE + step)
+
     def between():
         if pending:
             i, t = pending[0]
-            j = t - sp
-
-            @pl.when((sp > 0) & (j >= 0) & (j < pieces))
-            def _():
-                chain_step(i, j)
-
+            paced(i, t)
             pending[0] = (i, t + 1)
 
     def finish():
         if pending:
             i, t = pending.pop()
 
-            @pl.loop(t, pieces + sp_count - 1)
+            @pl.loop(t, pieces // PACE + sp_count - 1)
             def _(t):
-                j = t - sp
-
-                @pl.when((sp > 0) & (j >= 0) & (j < pieces))
-                def _():
-                    chain_step(i, j)
+                paced(i, t)
+
+    def chain_part(i, p):
+        @pl.loop(p * ROW_BLOCKS, (p + 1) * ROW_BLOCKS)
+        def _(j):
+            chain_step(i, j)
 
     for p in range(2):
         own_terms(0, p)
@@ -291,34 +329,33 @@
                     pass_on(i + 1, 0)
                 called.append(1)
 
-            invert(i, early)
-            finish()
-
-            @pl.when(sp == 0)
-            def _():
-                @pl.loop(0, pieces)
-                def _(j):
-                    chain_step(i, j)
-
+            def emit(p, i=i):
+                if p == 0:
+                    finish()
+                pl.when(sp == 0)(lambda: chain_part(i, p))
+
+            invert(i, early, emit)
             pending.append((i, 1))
         else:
-            invert(i, between)
-            finish()
-
-            @pl.loop(0, pieces)
-            def _(j):
-                chain_step(i, j)
+
+            def emit(p, i=i):
+                if p == 0:
+                    finish()
+                chain_part(i, p)
+
+            invert(i, between, emit)
 
     for p in range(2):
         pl.when(en < en_count - 1)(lambda p=p: halo_up(p).wait_send())
         pl.when(en > 0)(lambda p=p: halo_down(p).wait_send())
     for i in range(energy_count):
         for p in range(2):
-            to_ahead(i, p).wait_send()
-            if ring:
-                to_back(i, p).wait_send()
-            to_sibling(i, p).wait_send()
-            passing(i, p).wait_send()
+            for h in range(SHARES):
+                to_ahead(i, p, h).wait_send()
+                if ring:
+                    to_back(i, p, h).wait_send()
+                to_sibling(i, p, h).wait_send()
+                passing(i, p, h).wait_send()
 
         @pl.when(sp < sp_count - 1)
         def _():
@@ -333,15 +370,23 @@
     blocks = (energy_count, 2, n, n)
     slots = 4 if sizes[0] > 2 * REACH else 3
     pieces = 2 * ROW_BLOCKS
-    smem = pl.BlockSpec(memory_space=pltpu.SMEM)
+    hbm = pl.BlockSpec(memory_space=pltpu.HBM)
     vmem = pl.BlockSpec(memory_space=pltpu.VMEM)
     half = pltpu.VMEM((modes, n, n), jnp.bfloat16)
     out = pl.pallas_call(
         functools.partial(kernel, sizes),
         out_shape=jax.ShapeDtypeStruct(blocks, jnp.float32),
-        in_specs=[smem] * 4 + [vmem] * 4,
+        in_specs=[hbm] * 8,
         out_specs=vmem,
         scratch_shapes=[
+            pltpu.SMEM(mode_index.shape[1:], jnp.int32),
+            pltpu.SMEM(phonon_weight.shape, jnp.float32),
+            pltpu.SMEM((energy_count,), jnp.float32),
+            pltpu.SMEM((energy_count,), jnp.float32),
+            pltpu.VMEM(blocks, jnp.float32),
+            pltpu.VMEM(coupling.shape[1:], jnp.float32),
+            pltpu.VMEM((1, n), jnp.float32),
+            pltpu.VMEM((1, n), jnp.float32),
             pltpu.VMEM((2, 2, n, n), jnp.float32),
             pltpu.VMEM(blocks, jnp.float32),
             pltpu.VMEM((slots,) + blocks, jnp.float32),
@@ -350,15 +395,18 @@
             pltpu.VMEM(blocks, jnp.float32),
             pltpu.VMEM((n, n), jnp.float32),
             half, half, half, half,
+            pltpu.SemaphoreType.DMA((6,)),
+            pltpu.SemaphoreType.DMA,
+            pltpu.SemaphoreType.DMA((energy_count, 2)),
             pltpu.SemaphoreType.DMA((2, 2)),
             pltpu.SemaphoreType.DMA((2, 2)),
-            pltpu.SemaphoreType.DMA((slots, energy_count, 2)),
-            pltpu.SemaphoreType.DMA((slots, energy_count, 2)),
+            pltpu.SemaphoreType.DMA((slots, energy_count, 2, SHARES)),
+            pltpu.SemaphoreType.DMA((slots, energy_count, 2, SHARES)),
             pltpu.SemaphoreType.DMA((energy_count, pieces)),
             pltpu.SemaphoreType.DMA((energy_count, pieces)),
         ],
         compiler_params=pltpu.CompilerParams(
-            collective_id=0, has_side_effects=True, vmem_limit_bytes=50 << 20
+            collective_id=0, has_side_effects=True, vmem_limit_bytes=67_043_328
         ),
     )(
         mode_index[0], phonon_weight, energies, guess_scale.reshape(energy_count),

time: 57.4 us -> 55.5 us (0.967)
  local copies, waits for them, and re-layouts: 4.04 us -> 2.29 us
    unnamed x17 -> x1, local copies, waits for them, and re-layouts: 4.04 us -> 2.29 us
where the time goes in v2:
time: 55.5 us; the launch traced here: 55.3 us
  Pallas kernels  53 us (95%)
  local copies, waits for them, and re-layouts  2.29 us (4%)
    pallas_call x1, Pallas kernels, body(): pl.pallas_call(functools.partial(kernel, sizes), out_shape=jax.ShapeDtype...  53 us
    unnamed x1, local copies, waits for them, and re-layouts  2.29 us

profile of v2, /device:TPU:24, one launch (start us, length us, event | category | flops | bytes accessed | tf_op | source)
XLA Modules:
  0.0 55.3 jit_solution(14532228634928940212)
XLA Ops:
  0.0 53.0 %shard_map.82 = f32[2,2,256,256]{3,2,1,0:T(8,128)} custom-call(s32[5]{0:T(128)} %bitcast.10, f32[3]{0:T(128)} %weight_in.1, f32[2]{0:T(128)} %energy_in.1, f32[2]{0:T(128)} %bitcast.11, f32[2,2,256,256]{3,2,1,0:T(8,128)} %bitcast.8, f32[3,256,256]{2,1,0:T(8,128)} %bitcast.9, f32[1,256]{1,0:T(1,128)} %onsite_in.1, f32[1,256]{1,0:T(1,128)} %hopping_in.1), custom_call_target="tpu_custom_call" | custom-call | tf_op jit(solution)/shard_map/pallas_call | solution.py:376
  53.0 2.3 %copy.11 = f32[1,2,1,2,256,256]{5,4,3,2,1,0:T(8,128)} copy(f32[1,2,1,2,256,256]{5,4,3,2,1,0:T(8,128)} %bitcast.7) | data formatting | bytes 2097152

commit v3 on v2

--- a/solution.py
+++ b/solution.py
@@ -11,6 +11,7 @@
 ROW_BLOCKS = 8
 SHARES = 2
 PACE = 2
+WAITING = 2
 MESH = pl.DeviceIdType.MESH
 
 SIBLING, BACK, PASSED, AHEAD = range(4)
@@ -311,6 +312,9 @@
         for p in range(2):
             if not last:
                 issue(i + 1, p)
+            if i > 0 and p == 1:
+                for _ in range(WAITING):
+                    between()
             if i == 0 or p == 1:
                 pass_on(i, p)
             if not last:
@@ -406,11 +410,16 @@
             pltpu.SemaphoreType.DMA((energy_count, pieces)),
         ],
         compiler_params=pltpu.CompilerParams(
-            collective_id=0, has_side_effects=True, vmem_limit_bytes=67_043_328
+            collective_id=0, has_side_effects=True, vmem_limit_bytes=50 << 20
         ),
     )(
-        mode_index[0], phonon_weight, energies, guess_scale.reshape(energy_count),
-        green.reshape(blocks), coupling[0], onsite, hopping,
+        *(
+            pltpu.with_memory_space_constraint(value, pltpu.HBM)
+            for value in (
+                mode_index[0], phonon_weight, energies, guess_scale.reshape(energy_count),
+                green.reshape(blocks), coupling[0], onsite, hopping,
+            )
+        )
     )
     return out.reshape(1, energy_count, 1, 2, n, n)
 

time: 55.5 us -> 52.6 us (0.948)
  Pallas kernels: 53 us -> 51.5 us
  local copies, waits for them, and re-layouts: 2.29 us -> 0.97 us
    pallas_call x1, Pallas kernels: 53 us -> 51.5 us  [body(): pl.pallas_call(functools.partial(kernel, sizes), out_shape=jax.ShapeDtype...]
    unnamed x1, local copies, waits for them, and re-layouts: 2.29 us -> 0.97 us
where the time goes in v3:
time: 52.6 us; the launch traced here: 52.5 us
  Pallas kernels  51.5 us (98%)
  local copies, waits for them, and re-layouts  0.97 us (2%)
    pallas_call x1, Pallas kernels, body(): pl.pallas_call(functools.partial(kernel, sizes), out_shape=jax.ShapeDtype...  51.5 us

profile of v3, /device:TPU:24, one launch (start us, length us, event | category | flops | bytes accessed | tf_op | source)
XLA Modules:
  0.0 52.5 jit_solution(2198626889769413534)
XLA Ops:
  0.0 51.5 %shard_map.82 = f32[2,2,256,256]{3,2,1,0:T(8,128)S(1)} custom-call(s32[5]{0:T(128)} %bitcast.10, f32[3]{0:T(128)} %weight_in.1, f32[2]{0:T(128)} %energy_in.1, f32[2]{0:T(128)} %bitcast.11, f32[2,2,256,256]{3,2,1,0:T(8,128)} %bitcast.8, f32[3,256,256]{2,1,0:T(8,128)} %bitcast.9, f32[1,256]{1,0:T(1,128)} %onsite_in.1, f32[1,256]{1,0:T(1,128)} %hopping_in.1), custom_call_target="tpu_custom_call" | custom-call | tf_op jit(solution)/shard_map/pallas_call | solution.py:380
  51.5 1.0 %copy.11 = f32[1,2,1,2,256,256]{5,4,3,2,1,0:T(8,128)} copy(f32[1,2,1,2,256,256]{5,4,3,2,1,0:T(8,128)S(1)} %bitcast.7) | data formatting | bytes 2097152
